TPU v7x, 32 devices: a whole 2x2x4 slice. The times are simulated.
32 devices in a mesh: gz: 16 (over z, y, core), ta: 2 (over x).
Axes of the slice: x: 2, y: 2, z: 4, core: 2. Of those that a mesh axis runs over, the one named last changes fastest.
Arguments:
- outputs_fwd: bfloat16 [4, 32, 64, 1280], P('ta', 'gz'), may hold values from -6 to 6
- cotangent: bfloat16 [4, 32, 64, 1280], P('ta', 'gz'), may hold values from -6 to 6
- spatial_weight: bfloat16 [3, 64, 288], replicated, may hold values from -0.21875 to 0.21875
- hidden_bias: float32 [64], replicated, may hold values from -1 to 1
- temporal_weight: bfloat16 [3, 32, 64], replicated, may hold values from -0.4375 to 0.4375
Outputs:
- rebuilt: bfloat16 [4, 32, 32, 1280], P('ta', 'gz')
- grad_in: bfloat16 [4, 32, 32, 1280], P('ta', 'gz')
- grad_spatial: float32 [3, 64, 288], replicated
- grad_bias: float32 [64], replicated
- grad_temporal: float32 [3, 32, 64], replicated
All inputs are finite; a program needn't handle non-finite values.
Results may differ from a plain program's by a relative error of at most 0.0075.
Values may be sent and summed in bfloat16 or wider, within the bound.
A program may use at most 64 MiB of HBM per device.

v0:
```python
import math
import jax
import jax.numpy as jnp
from jax import lax
from jax.sharding import PartitionSpec as P

ROWS = 8
COLS = 160


def with_halo(cells, sides, width, closed):
    for axis, dim in sides:
        count = lax.axis_size(axis)
        ends = count if closed else count - 1
        head = lax.slice_in_dim(cells, 0, width, axis=dim)
        tail = lax.slice_in_dim(cells, cells.shape[dim] - width, cells.shape[dim], axis=dim)
        cells = jnp.concatenate(
            [
                lax.ppermute(tail, axis, [(i, (i + 1) % count) for i in range(ends)]),
                cells,
                lax.ppermute(head, axis, [((i + 1) % count, i) for i in range(ends)]),
            ],
            axis=dim,
        )
    return cells


def unfold(field):
    leading = field.shape[:-1]
    planar = field.reshape(leading + (ROWS, COLS))
    padded = jnp.pad(planar, [(0, 0)] * len(leading) + [(1, 1), (1, 1)])
    windows = [
        padded[..., row_off : row_off + ROWS, col_off : col_off + COLS]
        for row_off in range(3)
        for col_off in range(3)
    ]
    stacked = jnp.stack(windows, axis=-4)
    return stacked.reshape(leading[:-1] + (9 * leading[-1], ROWS * COLS))


def spatial(columns, spatial_weight, plane_count):
    total = jnp.einsum(
        "oi,fzir->fzor",
        spatial_weight[0],
        columns[:, 0:plane_count],
        preferred_element_type=jnp.float32,
    )
    total = total + jnp.einsum(
        "oi,fzir->fzor",
        spatial_weight[1],
        columns[:, 1 : plane_count + 1],
        preferred_element_type=jnp.float32,
    )
    total = total + jnp.einsum(
        "oi,fzir->fzor",
        spatial_weight[2],
        columns[:, 2 : plane_count + 2],
        preferred_element_type=jnp.float32,
    )
    return total


def temporal_back(temporal_weight, grad_around, frame_count):
    through = jnp.einsum(
        "oi,fzor->fzir",
        temporal_weight[0],
        grad_around[2 : frame_count + 2],
        preferred_element_type=jnp.float32,
    )
    through = through + jnp.einsum(
        "oi,fzor->fzir",
        temporal_weight[1],
        grad_around[1 : frame_count + 1],
        preferred_element_type=jnp.float32,
    )
    through = through + jnp.einsum(
        "oi,fzor->fzir",
        temporal_weight[2],
        grad_around[0:frame_count],
        preferred_element_type=jnp.float32,
    )
    return through


def hidden_gradient(through, hidden_in):
    sigmoid_val = jax.nn.sigmoid(hidden_in)
    return (through * sigmoid_val * (1.0 + hidden_in * (1.0 - sigmoid_val))).astype(jnp.bfloat16)


def shards(outputs_fwd, cotangent, spatial_weight, hidden_bias, temporal_weight):
    half = spatial_weight.shape[2] // 9
    hidden_count = spatial_weight.shape[1]
    front_half = outputs_fwd[:, :, :half]
    back_half = outputs_fwd[:, :, half:]
    grad_front = cotangent[:, :, :half]
    grad_back = cotangent[:, :, half:]
    frame_count = front_half.shape[0]
    plane_count = front_half.shape[1]
    bias_row = hidden_bias[None, None, :, None]
    depth_rim = 1
    padded_wide = with_halo(front_half, (("gz", 1),), depth_rim, False)
    columns = unfold(padded_wide)
    hidden_in = spatial(columns, spatial_weight, plane_count) + bias_row
    active = jax.nn.silu(hidden_in).astype(jnp.bfloat16)
    beside_all = with_halo(active, (("ta", 0),), 1, True)
    mapped = jnp.einsum(
        "oi,fzir->fzor",
        temporal_weight[0],
        beside_all[0:frame_count],
        preferred_element_type=jnp.float32,
    )
    mapped = mapped + jnp.einsum(
        "oi,fzir->fzor",
        temporal_weight[1],
        beside_all[1 : frame_count + 1],
        preferred_element_type=jnp.float32,
    )
    mapped = mapped + jnp.einsum(
        "oi,fzir->fzor",
        temporal_weight[2],
        beside_all[2 : frame_count + 2],
        preferred_element_type=jnp.float32,
    )
    rebuilt = (back_half.astype(jnp.float32) - mapped).astype(jnp.bfloat16)
    grad_around = with_halo(grad_back, (("ta", 0),), 1, True)
    through = temporal_back(temporal_weight, grad_around, frame_count)
    temporal_grad = jnp.stack(
        [
            jnp.einsum(
                "fzor,fzir->oi",
                grad_back,
                beside_all[offset : offset + frame_count],
                preferred_element_type=jnp.float32,
            )
            for offset in range(3)
        ]
    )
    hidden_grad = hidden_gradient(through, hidden_in)
    spatial_grad = jnp.stack(
        [
            jnp.einsum(
                "fzor,fzir->oi",
                hidden_grad,
                columns[:, depth : depth + plane_count],
                preferred_element_type=jnp.float32,
            )
            for depth in range(3)
        ]
    )
    bias_grad = jnp.einsum("fzor->o", hidden_grad.astype(jnp.float32))
    grad_planes = with_halo(hidden_grad, (("gz", 1),), 1, False)
    flipped = (
        spatial_weight.reshape((3, hidden_count, 9, half))[:, :, ::-1]
        .transpose((0, 3, 2, 1))
        .reshape((3, half, 9 * hidden_count))
    )

    def adjoint_frame(frame_planes):
        grad_columns = unfold(frame_planes)
        total = jnp.einsum(
            "ci,zir->zcr",
            flipped[0],
            grad_columns[2 : plane_count + 2],
            preferred_element_type=jnp.float32,
        )
        total = total + jnp.einsum(
            "ci,zir->zcr",
            flipped[1],
            grad_columns[1 : plane_count + 1],
            preferred_element_type=jnp.float32,
        )
        total = total + jnp.einsum(
            "ci,zir->zcr",
            flipped[2],
            grad_columns[0:plane_count],
            preferred_element_type=jnp.float32,
        )
        return total

    input_grad = lax.map(adjoint_frame, grad_planes)
    grad_in = (grad_front.astype(jnp.float32) + input_grad).astype(jnp.bfloat16)
    totals = lax.psum((spatial_grad, bias_grad, temporal_grad), ("gz", "ta"))
    factor = 1.0 / math.sqrt(
        frame_count * lax.axis_size("ta") * plane_count * lax.axis_size("gz") * ROWS * COLS
    )
    return (rebuilt, grad_in, totals[0] * factor, totals[1] * factor, totals[2] * factor)


def solution(mesh):
    placed = (P("ta", "gz", None, None), P("ta", "gz", None, None), P(), P(), P())
    return jax.shard_map(
        shards,
        mesh=mesh,
        in_specs=placed,
        out_specs=(P("ta", "gz", None, None), P("ta", "gz", None, None), P(), P(), P()),
        check_vma=False,
    )
```

profile of v0, /device:TPU:0, one launch (start us, length us, event | category | flops | bytes accessed | tf_op | source)
XLA Modules:
  0.0 338.4 jit_solution(7033846811327867473)
XLA Ops:
  7.2 1.1 fusion.125
  8.3 2.4 collective-permute-start
  10.8 1.3 collective-permute-start.1
  12.1 1.7 fusion.123
  13.7 2.3 collective-permute-start.4
  16.1 1.7 slice.236
  17.8 1.1 copy.41
  19.3 1.4 fusion.99
  20.8 1.3 reshape.45
  22.1 1.3 stack.118
  23.5 1.5 fusion.56
  25.0 1.2 fusion.58
  26.2 1.6 fusion.60
  27.8 1.4 fusion.62
  29.3 1.0 bitcast_dynamic-update-slice_fusion
  30.3 1.4 fusion.64
  31.7 1.7 fusion.66
  33.4 1.2 fusion.68
  34.6 1.6 fusion.70
  36.2 15.8 %reshape.46 = bf16[2,4,288,1280]{3,2,1,0:T(8,128)(2,1)} reshape(bf16[2,4,9,32,8,160]{5,4,3,2,1,0:T(8,128)(2,1)} %fusion.70) | data formatting | bytes 11796480 | tf_op jit(solution)/shard_map/reshape | solution.py:38
  52.0 2.7 fusion.40
  54.7 2.6 convolution_add_fusion.4
  57.4 0.9 multiply_convert_fusion
  58.4 1.5 fusion.87
  59.9 1.8 convert_reduce_fusion
  61.7 1.1 fusion.49
  62.8 1.1 fusion.46
  63.9 1.1 fusion.52
  65.1 1.1 fusion.101
  66.1 0.9 fusion.124
  67.0 0.7 pad_maximum_fusion.2
  67.8 4.3 %collective-permute-start.6 = (bf16[2,1,64,1280]{3,2,1,0:T(8,128)(2,1)S(1)}, bf16[2,1,64,1280]{3,2,1,0:T(8,128)(2,1)S(1)}, u32[]{:S(2)}, u32[]{:S(2)}) collective-permute-start(bf16[2,1,64,1280]{3,2,1,0:T(8,128)(2,1)S(1)} %get-tuple-element.72), channel_id=1, source_target_pairs={{0,2},{2,4},{4,6},{6,8},{8,10},{10,12},{12,14},{14,16},{16,18},{18... | collective-permute-start | bytes 983048 | tf_op jit(solution)/shard_map/ppermute | solution.py:19
  72.1 1.3 collective-permute-start.7
  73.4 1.6 collective-permute-start.2
  75.8 124.2 %all-reduce.5.cloned.1.call-done = f32[3,64,288]{2,1,0:T(8,128)} async-done(((f32[3,64,288]{2,1,0:T(8,128)}), f32[3,64,288]{2,1,0:T(8,128)}) %all-reduce.5.cloned.1.call-update) | async-done | bytes 221200 | tf_op jit(solution)/shard_map/psum | solution.py:182
  200.0 1.7 broadcast_multiply_fusion
  201.7 1.2 pad_maximum_fusion
  202.9 77.5 %while.12 = (s32[]{:T(128)}, f32[2,2,32,1280]{3,2,1,0:T(8,128)}, bf16[2,4,64,1280]{3,2,1,0:T(8,128)(2,1)}, bf16[3,32,576]{2,1,0:T(8,128)(2,1)S(1)}, s32[]{:T(128)}) while((s32[]{:T(128)}, f32[2,2,32,1280]{3,2,1,0:T(8,128)}, bf16[2,4,64,1280]{3,2,1,0:T(8,128)(2,1)}, bf16[3,32,576]{2,1,0:T(8,128)(2,1)S(1)}, s32[]{:T(128)}) %tuple.40), condition=%wide.region_1.2_spmd, body=%wide.region_0.1_spmd.sunk | while | flops 283279360 | bytes 69722216 | solution.py:180
  202.9 1.1 constant_dynamic-slice_fusion.2
  204.1 1.3 reshape.65
  205.4 1.3 stack.133
  209.1 0.8 fusion.162
  210.7 5.4 %fusion.165 = (bf16[2,9,64,8,160]{4,3,2,1,0:T(8,128)(2,1)}, bf16[2,9,64,8,160]{4,3,2,1,0:T(8,128)(2,1)}, bf16[2,9,64,8,160]{4,3,2,1,0:T(8,128)(2,1)}) fusion(bf16[4,9,64,8,160]{4,3,2,1,0:T(8,128)(2,1)S(1)} %fusion.164), kind=kLoop, calls=%fused_computation.155.clone.1 | loop fusion | bytes 17694720 | tf_op jit(solution)/shard_map/while/body/eval_jaxpr/slice | solution.py:175
  216.1 7.4 %slice.457 = bf16[2,576,1280]{2,1,0:T(8,128)(2,1)S(1)} reshape(bf16[2,9,64,8,160]{4,3,2,1,0:T(8,128)(2,1)} %get-tuple-element.112) | data formatting | bytes 5898240 | tf_op jit(solution)/shard_map/while/body/eval_jaxpr/slice | solution.py:163
  224.1 7.4 %slice.458 = bf16[2,576,1280]{2,1,0:T(8,128)(2,1)S(1)} reshape(bf16[2,9,64,8,160]{4,3,2,1,0:T(8,128)(2,1)} %get-tuple-element.113) | data formatting | bytes 5898240 | tf_op jit(solution)/shard_map/while/body/eval_jaxpr/slice | solution.py:169
  231.5 1.3 convolution_add_fusion.7
  232.9 7.4 %slice.459 = bf16[2,576,1280]{2,1,0:T(8,128)(2,1)S(1)} reshape(bf16[2,9,64,8,160]{4,3,2,1,0:T(8,128)(2,1)} %get-tuple-element.114) | data formatting | bytes 5898240 | tf_op jit(solution)/shard_map/while/body/eval_jaxpr/slice | solution.py:175
  240.4 1.4 fusion.167
  241.7 1.1 constant_dynamic-slice_fusion.2
  242.8 1.3 reshape.65
  244.2 1.3 stack.133
  247.8 0.8 fusion.162
  249.5 5.4 %fusion.165 = (bf16[2,9,64,8,160]{4,3,2,1,0:T(8,128)(2,1)}, bf16[2,9,64,8,160]{4,3,2,1,0:T(8,128)(2,1)}, bf16[2,9,64,8,160]{4,3,2,1,0:T(8,128)(2,1)}) fusion(bf16[4,9,64,8,160]{4,3,2,1,0:T(8,128)(2,1)S(1)} %fusion.164), kind=kLoop, calls=%fused_computation.155.clone.1 | loop fusion | bytes 17694720 | tf_op jit(solution)/shard_map/while/body/eval_jaxpr/slice | solution.py:175
  254.9 7.4 %slice.457 = bf16[2,576,1280]{2,1,0:T(8,128)(2,1)S(1)} reshape(bf16[2,9,64,8,160]{4,3,2,1,0:T(8,128)(2,1)} %get-tuple-element.112) | data formatting | bytes 5898240 | tf_op jit(solution)/shard_map/while/body/eval_jaxpr/slice | solution.py:163
  262.9 7.4 %slice.458 = bf16[2,576,1280]{2,1,0:T(8,128)(2,1)S(1)} reshape(bf16[2,9,64,8,160]{4,3,2,1,0:T(8,128)(2,1)} %get-tuple-element.113) | data formatting | bytes 5898240 | tf_op jit(solution)/shard_map/while/body/eval_jaxpr/slice | solution.py:169
  270.3 1.3 convolution_add_fusion.7
  271.7 7.4 %slice.459 = bf16[2,576,1280]{2,1,0:T(8,128)(2,1)S(1)} reshape(bf16[2,9,64,8,160]{4,3,2,1,0:T(8,128)(2,1)} %get-tuple-element.114) | data formatting | bytes 5898240 | tf_op jit(solution)/shard_map/while/body/eval_jaxpr/slice | solution.py:175
  279.1 1.3 fusion.167
  280.5 2.1 add_convert_fusion
  282.6 1.5 convolution_bitcast_fusion.1
  284.0 1.5 convolution_bitcast_fusion
  285.5 41.7 %all-reduce.2 = (f32[64]{0:T(128)S(1)}, f32[3,32,64]{2,1,0:T(8,128)S(1)}) all-reduce(f32[64]{0:T(128)S(1)} %get-tuple-element.82, f32[3,32,64]{2,1,0:T(8,128)S(1)} %pad_maximum_fusion.3), channel_id=1, replica_groups=mesh['gz'=16,'ta'=2] {'gz','ta'}, use_global_device_ids=true, to_apply=%region_4.5 | all-reduce | flops 6208 | bytes 49664 | tf_op jit(solution)/shard_map/psum | solution.py:182
  328.4 1.2 fusion.77
  329.6 1.9 fusion.45
  (70 shorter events, 10.2 us)
Async XLA Ops:
  7.2 13.6 %slice-start = ((bf16[2,2,64,1280]{3,2,1,0:T(8,128)(2,1)}), bf16[2,2,32,1280]{3,2,1,0:T(8,128)(2,1)S(1)}, s32[]{:S(2)}) async-start(bf16[2,2,64,1280]{3,2,1,0:T(8,128)(2,1)} %param.7), calls=%async_computation.1 | async-start | bytes 655360 | tf_op jit(solution)/shard_map/slice | solution.py:93
  7.2 12.1 %copy-start.4 = (bf16[2,2,64,1280]{3,2,1,0:T(8,128)(2,1)S(1)}, bf16[2,2,64,1280]{3,2,1,0:T(8,128)(2,1)}, u32[]{:S(2)}) copy-start(bf16[2,2,64,1280]{3,2,1,0:T(8,128)(2,1)} %param.8) | copy-start | bytes 1966084
  7.2 12.1 %copy-start.11 = (bf16[3,32,64]{2,1,0:T(8,128)(2,1)S(1)}, bf16[3,32,64]{2,1,0:T(8,128)(2,1)}, u32[]{:S(2)}) copy-start(bf16[3,32,64]{2,1,0:T(8,128)(2,1)} %param.11) | copy-start | bytes 36868
  7.2 192.8 %all-reduce.5.cloned.1.call-start = ((), (), s32[]{:S(2)}) async-start(), calls=%async_computation | async-start | bytes 589824 | tf_op jit(solution)/shard_map/psum | solution.py:182
  8.3 12.4 %collective-permute-start = (bf16[2,1,32,1280]{3,2,1,0:T(8,128)(2,1)S(1)}, bf16[2,1,32,1280]{3,2,1,0:T(8,128)(2,1)S(1)}, u32[]{:S(2)}, u32[]{:S(2)}) collective-permute-start(bf16[2,1,32,1280]{3,2,1,0:T(8,128)(2,1)S(1)} %get-tuple-element.78), channel_id=1, source_target_pairs={{0,2},{2,4},{4,6},{6,8},{8,10},{10,12},{12,14},{14,16},{16,18},{18... | collective-permute-start | bytes 491528 | tf_op jit(solution)/shard_map/ppermute | solution.py:19
  10.8 10.0 %collective-permute-start.1 = (bf16[2,1,32,1280]{3,2,1,0:T(8,128)(2,1)S(1)}, bf16[2,1,32,1280]{3,2,1,0:T(8,128)(2,1)S(1)}, u32[]{:S(2)}, u32[]{:S(2)}) collective-permute-start(bf16[2,1,32,1280]{3,2,1,0:T(8,128)(2,1)S(1)} %get-tuple-element.79), channel_id=1, source_target_pairs={{2,0},{4,2},{6,4},{8,6},{10,8},{12,10},{14,12},{16,14},{18,16},{20... | collective-permute-start | bytes 491528 | tf_op jit(solution)/shard_map/ppermute | solution.py:21
  13.7 46.1 %collective-permute-start.4 = (bf16[1,2,32,1280]{3,2,1,0:T(8,128)(2,1)}, bf16[1,2,32,1280]{3,2,1,0:T(8,128)(2,1)}, u32[]{:S(2)}, u32[]{:S(2)}) collective-permute-start(bf16[1,2,32,1280]{3,2,1,0:T(8,128)(2,1)} %get-tuple-element.74), channel_id=1, source_target_pairs={{1,0},{0,1},{3,2},{2,3},{5,4},{4,5},{7,6},{6,7},{9,8},{8,9},{11,10... | collective-permute-start | bytes 491528 | tf_op jit(solution)/shard_map/ppermute | solution.py:21
  16.1 42.3 %collective-permute-start.5 = (bf16[1,2,32,1280]{3,2,1,0:T(8,128)(2,1)S(1)}, bf16[1,2,32,1280]{3,2,1,0:T(8,128)(2,1)}, u32[]{:S(2)}, u32[]{:S(2)}) collective-permute-start(bf16[1,2,32,1280]{3,2,1,0:T(8,128)(2,1)S(1)} %get-tuple-element.75), channel_id=1, source_target_pairs={{0,1},{1,0},{2,3},{3,2},{4,5},{5,4},{6,7},{7,6},{8,9},{9,8},{10,11... | collective-permute-start | bytes 491528 | tf_op jit(solution)/shard_map/ppermute | solution.py:19
  36.2 15.8 %copy-start.10 = (bf16[3,64,288]{2,1,0:T(8,128)(2,1)S(1)}, bf16[3,64,288]{2,1,0:T(8,128)(2,1)}, u32[]{:S(2)}) copy-start(bf16[3,64,288]{2,1,0:T(8,128)(2,1)} %param.9) | copy-start | bytes 331780
  52.0 5.4 %copy-start.1 = (bf16[2,4,288,1280]{3,2,1,0:T(8,128)(2,1)S(1)}, bf16[2,4,288,1280]{3,2,1,0:T(8,128)(2,1)}, u32[]{:S(2)}) copy-start(bf16[2,4,288,1280]{3,2,1,0:T(8,128)(2,1)} %reshape.46) | copy-start | bytes 17694724
  54.7 2.7 copy-start.12
  57.4 1.0 copy-start.8
  57.4 2.5 copy-start.9
  58.3 17.2 %copy-start.2 = (bf16[2,2,64,1280]{3,2,1,0:T(8,128)(2,1)}, bf16[2,2,64,1280]{3,2,1,0:T(8,128)(2,1)S(1)}, u32[]{:S(2)}) copy-start(bf16[2,2,64,1280]{3,2,1,0:T(8,128)(2,1)S(1)} %get-tuple-element.80) | copy-start | bytes 1966084
  65.0 10.5 %copy-start.5 = (bf16[2,2,64,1280]{3,2,1,0:T(8,128)(2,1)S(1)}, bf16[2,2,64,1280]{3,2,1,0:T(8,128)(2,1)}, u32[]{:S(2)}) copy-start(bf16[2,2,64,1280]{3,2,1,0:T(8,128)(2,1)} %param.8) | copy-start | bytes 1966084
  67.8 133.9 %collective-permute-start.6 = (bf16[2,1,64,1280]{3,2,1,0:T(8,128)(2,1)S(1)}, bf16[2,1,64,1280]{3,2,1,0:T(8,128)(2,1)S(1)}, u32[]{:S(2)}, u32[]{:S(2)}) collective-permute-start(bf16[2,1,64,1280]{3,2,1,0:T(8,128)(2,1)S(1)} %get-tuple-element.72), channel_id=1, source_target_pairs={{0,2},{2,4},{4,6},{6,8},{8,10},{10,12},{12,14},{14,16},{16,18},{18... | collective-permute-start | bytes 983048 | tf_op jit(solution)/shard_map/ppermute | solution.py:19
  72.1 129.6 %collective-permute-start.7 = (bf16[2,1,64,1280]{3,2,1,0:T(8,128)(2,1)S(1)}, bf16[2,1,64,1280]{3,2,1,0:T(8,128)(2,1)S(1)}, u32[]{:S(2)}, u32[]{:S(2)}) collective-permute-start(bf16[2,1,64,1280]{3,2,1,0:T(8,128)(2,1)S(1)} %get-tuple-element.73), channel_id=1, source_target_pairs={{2,0},{4,2},{6,4},{8,6},{10,8},{12,10},{14,12},{16,14},{18,16},{20... | collective-permute-start | bytes 983048 | tf_op jit(solution)/shard_map/ppermute | solution.py:21
  73.4 209.2 %collective-permute-start.2 = (bf16[1,2,64,1280]{3,2,1,0:T(8,128)(2,1)}, bf16[1,2,64,1280]{3,2,1,0:T(8,128)(2,1)}, u32[]{:S(2)}, u32[]{:S(2)}) collective-permute-start(bf16[1,2,64,1280]{3,2,1,0:T(8,128)(2,1)} %get-tuple-element.76), channel_id=1, source_target_pairs={{0,1},{1,0},{2,3},{3,2},{4,5},{5,4},{6,7},{7,6},{8,9},{9,8},{10,11... | collective-permute-start | bytes 983048 | tf_op jit(solution)/shard_map/ppermute | solution.py:19
  75.0 209.1 %collective-permute-start.3 = (bf16[1,2,64,1280]{3,2,1,0:T(8,128)(2,1)}, bf16[1,2,64,1280]{3,2,1,0:T(8,128)(2,1)}, u32[]{:S(2)}, u32[]{:S(2)}) collective-permute-start(bf16[1,2,64,1280]{3,2,1,0:T(8,128)(2,1)} %get-tuple-element.77), channel_id=1, source_target_pairs={{1,0},{0,1},{3,2},{2,3},{5,4},{4,5},{7,6},{6,7},{9,8},{8,9},{11,10... | collective-permute-start | bytes 983048 | tf_op jit(solution)/shard_map/ppermute | solution.py:21
  232.9 7.5 %copy-start = (f32[2,1280,32]{1,2,0:T(8,128)S(1)}, f32[2,1280,32]{1,2,0:T(8,128)}, u32[]{:S(2)}) copy-start(f32[2,1280,32]{1,2,0:T(8,128)} %convolution_add_fusion.7) | copy-start | bytes 983044 | tf_op jit(solution)/shard_map/while
  271.6 7.5 %copy-start = (f32[2,1280,32]{1,2,0:T(8,128)S(1)}, f32[2,1280,32]{1,2,0:T(8,128)}, u32[]{:S(2)}) copy-start(f32[2,1280,32]{1,2,0:T(8,128)} %convolution_add_fusion.7) | copy-start | bytes 983044 | tf_op jit(solution)/shard_map/while
  280.5 47.9 %copy-start.3 = (bf16[2,2,64,1280]{3,2,1,0:T(8,128)(2,1)S(1)}, bf16[2,2,64,1280]{3,2,1,0:T(8,128)(2,1)}, u32[]{:S(2)}) copy-start(bf16[2,2,64,1280]{3,2,1,0:T(8,128)(2,1)} %copy-done.2) | copy-start | bytes 1966084
  280.5 49.1 %copy-start.6 = (f32[2,2,1280,32]{2,3,1,0:T(8,128)S(1)}, f32[2,2,1280,32]{2,3,1,0:T(8,128)}, u32[]{:S(2)}) copy-start(f32[2,2,1280,32]{2,3,1,0:T(8,128)} %fusion.101) | copy-start | bytes 1966084
  280.5 49.1 %copy-start.7 = (bf16[2,2,64,1280]{3,2,1,0:T(8,128)(2,1)S(1)}, bf16[2,2,64,1280]{3,2,1,0:T(8,128)(2,1)}, u32[]{:S(2)}) copy-start(bf16[2,2,64,1280]{3,2,1,0:T(8,128)(2,1)} %param.7) | copy-start | bytes 1966084
Sparse Core Ops, SparseCore 0:
  67.9 132.0 all-reduce.4
where the time goes:
time: 340 us; the launch traced here: 338 us
  waiting for transfers between devices  124 us (36%)
  local copies, waits for them, and re-layouts  109 us (32%)
  blocking collectives  41.7 us (12%)
  matrix products  28.3 us (8%)
  between operations  14.4 us (4%)
  starting transfers between devices  13.8 us (4%)
  other arithmetic  6.97 us (2%)
    psum x1, waiting for transfers between devices, shards(): totals = lax.psum((spatial_grad, bias_grad, temporal_grad), ('gz', 'ta'))  124 us
    psum x1, blocking collectives, shards(): totals = lax.psum((spatial_grad, bias_grad, temporal_grad), ('gz', 'ta'))  41.7 us
    slice x4, local copies, waits for them, and re-layouts, adjoint_frame(): grad_columns[0:plane_count]  25.7 us
    reshape x1, local copies, waits for them, and re-layouts, unfold(): return stacked.reshape(leading[:-1] + (9 * leading[-1], ROWS * COLS))  15.8 us
    slice x2, local copies, waits for them, and re-layouts, adjoint_frame(): grad_columns[1:plane_count + 1]  14.8 us
    slice x2, local copies, waits for them, and re-layouts, adjoint_frame(): grad_columns[2:plane_count + 2]  14.8 us
    unnamed x33, local copies, waits for them, and re-layouts  12.3 us
    ppermute x4, starting transfers between devices, with_halo(): lax.ppermute(tail, axis, [(i, (i + 1) % count) for i in range(ends)])  8.3 us
  transfers between devices with their start and end apart: 9, of which 1 were waited for; matrix products, arithmetic and copies ran while one was open for 38% of the time, Pallas kernels for 0%

commit v1 on v0

--- a/solution.py
+++ b/solution.py
@@ -179,7 +179,9 @@
 
     input_grad = lax.map(adjoint_frame, grad_planes)
     grad_in = (grad_front.astype(jnp.float32) + input_grad).astype(jnp.bfloat16)
-    totals = lax.psum((spatial_grad, bias_grad, temporal_grad), ("gz", "ta"))
+    totals = (spatial_grad, bias_grad, temporal_grad)
+    for num in ("ta", "gz"):
+        totals = jax.lax.psum(totals, num)
     factor = 1.0 / math.sqrt(
         frame_count * lax.axis_size("ta") * plane_count * lax.axis_size("gz") * ROWS * COLS
     )

time: 340 us -> 271 us (0.80)
  waiting for transfers between devices: 124 us -> 29.1 us
  blocking collectives: 41.7 us -> 67.2 us
    psum x1 -> x2, waiting for transfers between devices: 124 us -> 29 us  [shards(): totals = jax.lax.psum(totals, num)]
    psum x1 -> x2, blocking collectives: 41.7 us -> 67.2 us  [shards(): totals = jax.lax.psum(totals, num)]
  transfers between devices with their start and end apart: 9 -> 10, of which waited for: 1 -> 1; matrix products, arithmetic and copies ran while one was open for 38% -> 50% of each run, Pallas kernels for 0% -> 0%
where the time goes in v1:
time: 271 us; the launch traced here: 269 us
  local copies, waits for them, and re-layouts  109 us (40%)
  blocking collectives  67.2 us (25%)
  waiting for transfers between devices  29.1 us (11%)
  matrix products  28.3 us (10%)
  between operations  14.4 us (5%)
  starting transfers between devices  13.8 us (5%)
  other arithmetic  7 us (3%)
    psum x2, blocking collectives, shards(): totals = jax.lax.psum(totals, num)  67.2 us
    psum x2, waiting for transfers between devices, shards(): totals = jax.lax.psum(totals, num)  29 us
    slice x4, local copies, waits for them, and re-layouts, adjoint_frame(): grad_columns[0:plane_count]  26 us
    reshape x1, local copies, waits for them, and re-layouts, unfold(): return stacked.reshape(leading[:-1] + (9 * leading[-1], ROWS * COLS))  15.8 us
    slice x2, local copies, waits for them, and re-layouts, adjoint_frame(): grad_columns[1:plane_count + 1]  14.9 us
    slice x2, local copies, waits for them, and re-layouts, adjoint_frame(): grad_columns[2:plane_count + 2]  14.8 us
    unnamed x33, local copies, waits for them, and re-layouts  12.3 us
    ppermute x4, starting transfers between devices, with_halo(): lax.ppermute(tail, axis, [(i, (i + 1) % count) for i in range(ends)])  8.27 us
  transfers between devices with their start and end apart: 10, of which 1 were waited for; matrix products, arithmetic and copies ran while one was open for 50% of the time, Pallas kernels for 0%

profile of v1, /device:TPU:0, one launch (start us, length us, event | category | flops | bytes accessed | tf_op | source)
XLA Modules:
  0.0 269.0 jit_solution(12618710953479311593)
XLA Ops:
  7.2 1.1 fusion.125
  8.3 2.4 collective-permute-start
  10.8 1.3 collective-permute-start.1
  12.1 1.7 fusion.123
  13.7 2.3 collective-permute-start.4
  16.1 1.7 slice.236
  17.8 1.1 copy.41
  19.3 1.5 fusion.99
  20.8 1.3 reshape.45
  22.2 1.3 stack.118
  23.5 1.5 fusion.56
  25.0 1.3 fusion.58
  26.3 1.6 fusion.60
  27.8 1.4 fusion.62
  29.3 1.0 bitcast_dynamic-update-slice_fusion
  30.3 1.4 fusion.64
  31.7 1.7 fusion.66
  33.4 1.3 fusion.68
  34.7 1.6 fusion.70
  36.2 15.8 %reshape.46 = bf16[2,4,288,1280]{3,2,1,0:T(8,128)(2,1)} reshape(bf16[2,4,9,32,8,160]{5,4,3,2,1,0:T(8,128)(2,1)} %fusion.70) | data formatting | bytes 11796480 | tf_op jit(solution)/shard_map/reshape | solution.py:38
  52.0 2.7 %fusion.40 = f32[2,2,1280,64]{2,3,1,0:T(8,128)S(1)} fusion(bf16[2,4,288,1280]{3,2,1,0:T(8,128)(2,1)} %reshape.46, bf16[3,64,288]{2,1,0:T(8,128)(2,1)S(1)} %copy-done.10), kind=kOutput, calls=%fused_computation.63 | convolution fusion | flops 188743680 | bytes 4308992 | tf_op jit(solution)/shard_map/oi,fzir->fzor/dot_general | solution.py:42
  54.8 2.6 convolution_add_fusion.4
  57.5 0.9 multiply_convert_fusion
  58.4 1.5 fusion.87
  59.9 1.8 convert_reduce_fusion
  61.7 1.1 fusion.49
  62.8 1.1 fusion.46
  63.9 1.1 fusion.52
  65.4 0.9 fusion.124
  66.3 4.3 %collective-permute-start.6 = (bf16[2,1,64,1280]{3,2,1,0:T(8,128)(2,1)S(1)}, bf16[2,1,64,1280]{3,2,1,0:T(8,128)(2,1)S(1)}, u32[]{:S(2)}, u32[]{:S(2)}) collective-permute-start(bf16[2,1,64,1280]{3,2,1,0:T(8,128)(2,1)S(1)} %get-tuple-element.74), channel_id=1, source_target_pairs={{0,2},{2,4},{4,6},{6,8},{8,10},{10,12},{12,14},{14,16},{16,18},{18... | collective-permute-start | bytes 983048 | tf_op jit(solution)/shard_map/ppermute | solution.py:19
  70.6 1.3 collective-permute-start.7
  72.7 1.5 collective-permute-start.2
  74.8 1.1 fusion.101
  75.9 29.0 %all-reduce.7.cloned.1.call-done = f32[3,64,288]{2,1,0:T(8,128)} async-done(((f32[3,64,288]{2,1,0:T(8,128)}), f32[3,64,288]{2,1,0:T(8,128)}) %all-reduce.7.cloned.1.call-update) | async-done | bytes 221200 | tf_op jit(solution)/shard_map/psum | solution.py:184
  104.9 1.2 pad_maximum_fusion
  106.1 77.8 %while.12 = (s32[]{:T(128)}, f32[2,2,32,1280]{3,2,1,0:T(8,128)}, bf16[2,4,64,1280]{3,2,1,0:T(8,128)(2,1)}, bf16[3,32,576]{2,1,0:T(8,128)(2,1)S(1)}, s32[]{:T(128)}) while((s32[]{:T(128)}, f32[2,2,32,1280]{3,2,1,0:T(8,128)}, bf16[2,4,64,1280]{3,2,1,0:T(8,128)(2,1)}, bf16[3,32,576]{2,1,0:T(8,128)(2,1)S(1)}, s32[]{:T(128)}) %tuple.40), condition=%wide.region_1.2_spmd, body=%wide.region_0.1_spmd.sunk | while | flops 283279360 | bytes 69722216 | solution.py:180
  106.1 1.1 constant_dynamic-slice_fusion.2
  107.3 1.3 reshape.65
  108.6 1.3 stack.133
  112.2 0.8 fusion.162
  113.9 5.5 %fusion.165 = (bf16[2,9,64,8,160]{4,3,2,1,0:T(8,128)(2,1)}, bf16[2,9,64,8,160]{4,3,2,1,0:T(8,128)(2,1)}, bf16[2,9,64,8,160]{4,3,2,1,0:T(8,128)(2,1)}) fusion(bf16[4,9,64,8,160]{4,3,2,1,0:T(8,128)(2,1)S(1)} %fusion.164), kind=kLoop, calls=%fused_computation.155.clone.1 | loop fusion | bytes 17694720 | tf_op jit(solution)/shard_map/while/body/eval_jaxpr/slice | solution.py:175
  119.4 7.4 %slice.457 = bf16[2,576,1280]{2,1,0:T(8,128)(2,1)S(1)} reshape(bf16[2,9,64,8,160]{4,3,2,1,0:T(8,128)(2,1)} %get-tuple-element.114) | data formatting | bytes 5898240 | tf_op jit(solution)/shard_map/while/body/eval_jaxpr/slice | solution.py:163
  127.4 7.4 %slice.458 = bf16[2,576,1280]{2,1,0:T(8,128)(2,1)S(1)} reshape(bf16[2,9,64,8,160]{4,3,2,1,0:T(8,128)(2,1)} %get-tuple-element.115) | data formatting | bytes 5898240 | tf_op jit(solution)/shard_map/while/body/eval_jaxpr/slice | solution.py:169
  134.9 1.3 convolution_add_fusion.7
  136.2 7.5 %slice.459 = bf16[2,576,1280]{2,1,0:T(8,128)(2,1)S(1)} reshape(bf16[2,9,64,8,160]{4,3,2,1,0:T(8,128)(2,1)} %get-tuple-element.116) | data formatting | bytes 5898240 | tf_op jit(solution)/shard_map/while/body/eval_jaxpr/slice | solution.py:175
  143.7 1.4 fusion.167
  145.0 1.1 constant_dynamic-slice_fusion.2
  146.2 1.3 reshape.65
  147.5 1.3 stack.133
  151.1 0.8 fusion.162
  152.8 5.5 %fusion.165 = (bf16[2,9,64,8,160]{4,3,2,1,0:T(8,128)(2,1)}, bf16[2,9,64,8,160]{4,3,2,1,0:T(8,128)(2,1)}, bf16[2,9,64,8,160]{4,3,2,1,0:T(8,128)(2,1)}) fusion(bf16[4,9,64,8,160]{4,3,2,1,0:T(8,128)(2,1)S(1)} %fusion.164), kind=kLoop, calls=%fused_computation.155.clone.1 | loop fusion | bytes 17694720 | tf_op jit(solution)/shard_map/while/body/eval_jaxpr/slice | solution.py:175
  158.3 7.4 %slice.457 = bf16[2,576,1280]{2,1,0:T(8,128)(2,1)S(1)} reshape(bf16[2,9,64,8,160]{4,3,2,1,0:T(8,128)(2,1)} %get-tuple-element.114) | data formatting | bytes 5898240 | tf_op jit(solution)/shard_map/while/body/eval_jaxpr/slice | solution.py:163
  166.3 7.4 %slice.458 = bf16[2,576,1280]{2,1,0:T(8,128)(2,1)S(1)} reshape(bf16[2,9,64,8,160]{4,3,2,1,0:T(8,128)(2,1)} %get-tuple-element.115) | data formatting | bytes 5898240 | tf_op jit(solution)/shard_map/while/body/eval_jaxpr/slice | solution.py:169
  173.8 1.3 convolution_add_fusion.7
  175.1 7.5 %slice.459 = bf16[2,576,1280]{2,1,0:T(8,128)(2,1)S(1)} reshape(bf16[2,9,64,8,160]{4,3,2,1,0:T(8,128)(2,1)} %get-tuple-element.116) | data formatting | bytes 5898240 | tf_op jit(solution)/shard_map/while/body/eval_jaxpr/slice | solution.py:175
  182.6 1.3 fusion.167
  183.9 2.1 add_convert_fusion
  186.0 1.5 convolution_bitcast_fusion.1
  187.5 1.5 convolution_bitcast_fusion
  189.0 7.5 %all-reduce.3 = (f32[64]{0:T(128)S(1)}, f32[3,32,64]{2,1,0:T(8,128)S(1)}) all-reduce(f32[64]{0:T(128)S(1)} %get-tuple-element.84, f32[3,32,64]{2,1,0:T(8,128)S(1)} %pad_maximum_fusion.3), channel_id=1, replica_groups=mesh['gz'=16,'ta'=2] {'ta'}, use_global_device_ids=true, to_apply=%region_5.6 | all-reduce | flops 6208 | bytes 49664 | tf_op jit(solution)/shard_map/psum | solution.py:184
  196.5 59.6 %all-reduce.2 = (f32[64]{0:T(128)S(1)}, f32[3,32,64]{2,1,0:T(8,128)S(1)}) all-reduce(f32[64]{0:T(128)S(1)} %get-tuple-element.69, f32[3,32,64]{2,1,0:T(8,128)S(1)} %get-tuple-element.70), channel_id=1, replica_groups=mesh['gz'=16,'ta'=2] {'gz'}, use_global_device_ids=true, to_apply=%region_6.7 | all-reduce | flops 6208 | bytes 49664 | tf_op jit(solution)/shard_map/psum | solution.py:184
  256.8 1.2 fusion.77
  258.0 1.9 fusion.45
  260.5 1.7 broadcast_multiply_fusion
  (74 shorter events, 11.0 us)
Async XLA Ops:
  7.2 13.6 %slice-start = ((bf16[2,2,64,1280]{3,2,1,0:T(8,128)(2,1)}), bf16[2,2,32,1280]{3,2,1,0:T(8,128)(2,1)S(1)}, s32[]{:S(2)}) async-start(bf16[2,2,64,1280]{3,2,1,0:T(8,128)(2,1)} %param.7), calls=%async_computation.2 | async-start | bytes 655360 | tf_op jit(solution)/shard_map/slice | solution.py:93
  7.2 12.1 %copy-start.4 = (bf16[2,2,64,1280]{3,2,1,0:T(8,128)(2,1)S(1)}, bf16[2,2,64,1280]{3,2,1,0:T(8,128)(2,1)}, u32[]{:S(2)}) copy-start(bf16[2,2,64,1280]{3,2,1,0:T(8,128)(2,1)} %param.8) | copy-start | bytes 1966084
  7.2 12.1 %copy-start.11 = (bf16[3,32,64]{2,1,0:T(8,128)(2,1)S(1)}, bf16[3,32,64]{2,1,0:T(8,128)(2,1)}, u32[]{:S(2)}) copy-start(bf16[3,32,64]{2,1,0:T(8,128)(2,1)} %param.11) | copy-start | bytes 36868
  7.2 97.6 %all-reduce.7.cloned.1.call-start = ((), (), s32[]{:S(2)}) async-start(), calls=%async_computation | async-start | bytes 589824 | tf_op jit(solution)/shard_map/psum | solution.py:184
  8.3 12.4 %collective-permute-start = (bf16[2,1,32,1280]{3,2,1,0:T(8,128)(2,1)S(1)}, bf16[2,1,32,1280]{3,2,1,0:T(8,128)(2,1)S(1)}, u32[]{:S(2)}, u32[]{:S(2)}) collective-permute-start(bf16[2,1,32,1280]{3,2,1,0:T(8,128)(2,1)S(1)} %get-tuple-element.80), channel_id=1, source_target_pairs={{0,2},{2,4},{4,6},{6,8},{8,10},{10,12},{12,14},{14,16},{16,18},{18... | collective-permute-start | bytes 491528 | tf_op jit(solution)/shard_map/ppermute | solution.py:19
  10.8 10.0 %collective-permute-start.1 = (bf16[2,1,32,1280]{3,2,1,0:T(8,128)(2,1)S(1)}, bf16[2,1,32,1280]{3,2,1,0:T(8,128)(2,1)S(1)}, u32[]{:S(2)}, u32[]{:S(2)}) collective-permute-start(bf16[2,1,32,1280]{3,2,1,0:T(8,128)(2,1)S(1)} %get-tuple-element.81), channel_id=1, source_target_pairs={{2,0},{4,2},{6,4},{8,6},{10,8},{12,10},{14,12},{16,14},{18,16},{20... | collective-permute-start | bytes 491528 | tf_op jit(solution)/shard_map/ppermute | solution.py:21
  13.7 46.2 %collective-permute-start.4 = (bf16[1,2,32,1280]{3,2,1,0:T(8,128)(2,1)}, bf16[1,2,32,1280]{3,2,1,0:T(8,128)(2,1)}, u32[]{:S(2)}, u32[]{:S(2)}) collective-permute-start(bf16[1,2,32,1280]{3,2,1,0:T(8,128)(2,1)} %get-tuple-element.76), channel_id=1, source_target_pairs={{1,0},{0,1},{3,2},{2,3},{5,4},{4,5},{7,6},{6,7},{9,8},{8,9},{11,10... | collective-permute-start | bytes 491528 | tf_op jit(solution)/shard_map/ppermute | solution.py:21
  16.1 42.3 %collective-permute-start.5 = (bf16[1,2,32,1280]{3,2,1,0:T(8,128)(2,1)S(1)}, bf16[1,2,32,1280]{3,2,1,0:T(8,128)(2,1)}, u32[]{:S(2)}, u32[]{:S(2)}) collective-permute-start(bf16[1,2,32,1280]{3,2,1,0:T(8,128)(2,1)S(1)} %get-tuple-element.77), channel_id=1, source_target_pairs={{0,1},{1,0},{2,3},{3,2},{4,5},{5,4},{6,7},{7,6},{8,9},{9,8},{10,11... | collective-permute-start | bytes 491528 | tf_op jit(solution)/shard_map/ppermute | solution.py:19
  36.2 15.8 %copy-start.10 = (bf16[3,64,288]{2,1,0:T(8,128)(2,1)S(1)}, bf16[3,64,288]{2,1,0:T(8,128)(2,1)}, u32[]{:S(2)}) copy-start(bf16[3,64,288]{2,1,0:T(8,128)(2,1)} %param.9) | copy-start | bytes 331780
  52.0 5.4 %copy-start.1 = (bf16[2,4,288,1280]{3,2,1,0:T(8,128)(2,1)S(1)}, bf16[2,4,288,1280]{3,2,1,0:T(8,128)(2,1)}, u32[]{:S(2)}) copy-start(bf16[2,4,288,1280]{3,2,1,0:T(8,128)(2,1)} %reshape.46) | copy-start | bytes 17694724
  54.7 2.7 copy-start.12
  57.4 1.0 copy-start.8
  57.4 2.5 copy-start.9
  58.4 16.4 %copy-start.2 = (bf16[2,2,64,1280]{3,2,1,0:T(8,128)(2,1)}, bf16[2,2,64,1280]{3,2,1,0:T(8,128)(2,1)S(1)}, u32[]{:S(2)}) copy-start(bf16[2,2,64,1280]{3,2,1,0:T(8,128)(2,1)S(1)} %get-tuple-element.82) | copy-start | bytes 1966084
  63.9 1.2 copy-start.5
  66.3 38.6 %collective-permute-start.6 = (bf16[2,1,64,1280]{3,2,1,0:T(8,128)(2,1)S(1)}, bf16[2,1,64,1280]{3,2,1,0:T(8,128)(2,1)S(1)}, u32[]{:S(2)}, u32[]{:S(2)}) collective-permute-start(bf16[2,1,64,1280]{3,2,1,0:T(8,128)(2,1)S(1)} %get-tuple-element.74), channel_id=1, source_target_pairs={{0,2},{2,4},{4,6},{6,8},{8,10},{10,12},{12,14},{14,16},{16,18},{18... | collective-permute-start | bytes 983048 | tf_op jit(solution)/shard_map/ppermute | solution.py:19
  70.6 34.3 %collective-permute-start.7 = (bf16[2,1,64,1280]{3,2,1,0:T(8,128)(2,1)S(1)}, bf16[2,1,64,1280]{3,2,1,0:T(8,128)(2,1)S(1)}, u32[]{:S(2)}, u32[]{:S(2)}) collective-permute-start(bf16[2,1,64,1280]{3,2,1,0:T(8,128)(2,1)S(1)} %get-tuple-element.75), channel_id=1, source_target_pairs={{2,0},{4,2},{6,4},{8,6},{10,8},{12,10},{14,12},{16,14},{18,16},{20... | collective-permute-start | bytes 983048 | tf_op jit(solution)/shard_map/ppermute | solution.py:21
  72.6 187.8 %all-reduce.9.cloned.1.call-start = ((), (), s32[]{:S(2)}) async-start(), calls=%async_computation.1 | async-start | bytes 589824 | tf_op jit(solution)/shard_map/psum | solution.py:184
  72.7 113.4 %collective-permute-start.2 = (bf16[1,2,64,1280]{3,2,1,0:T(8,128)(2,1)}, bf16[1,2,64,1280]{3,2,1,0:T(8,128)(2,1)}, u32[]{:S(2)}, u32[]{:S(2)}) collective-permute-start(bf16[1,2,64,1280]{3,2,1,0:T(8,128)(2,1)} %get-tuple-element.78), channel_id=1, source_target_pairs={{0,1},{1,0},{2,3},{3,2},{4,5},{5,4},{6,7},{7,6},{8,9},{9,8},{10,11... | collective-permute-start | bytes 983048 | tf_op jit(solution)/shard_map/ppermute | solution.py:19
  74.2 113.3 %collective-permute-start.3 = (bf16[1,2,64,1280]{3,2,1,0:T(8,128)(2,1)}, bf16[1,2,64,1280]{3,2,1,0:T(8,128)(2,1)}, u32[]{:S(2)}, u32[]{:S(2)}) collective-permute-start(bf16[1,2,64,1280]{3,2,1,0:T(8,128)(2,1)} %get-tuple-element.79), channel_id=1, source_target_pairs={{1,0},{0,1},{3,2},{2,3},{5,4},{4,5},{7,6},{6,7},{9,8},{8,9},{11,10... | collective-permute-start | bytes 983048 | tf_op jit(solution)/shard_map/ppermute | solution.py:21
  136.2 7.5 %copy-start = (f32[2,1280,32]{1,2,0:T(8,128)S(1)}, f32[2,1280,32]{1,2,0:T(8,128)}, u32[]{:S(2)}) copy-start(f32[2,1280,32]{1,2,0:T(8,128)} %convolution_add_fusion.7) | copy-start | bytes 983044 | tf_op jit(solution)/shard_map/while
  175.1 7.5 %copy-start = (f32[2,1280,32]{1,2,0:T(8,128)S(1)}, f32[2,1280,32]{1,2,0:T(8,128)}, u32[]{:S(2)}) copy-start(f32[2,1280,32]{1,2,0:T(8,128)} %convolution_add_fusion.7) | copy-start | bytes 983044 | tf_op jit(solution)/shard_map/while
  183.9 72.9 %copy-start.3 = (bf16[2,2,64,1280]{3,2,1,0:T(8,128)(2,1)S(1)}, bf16[2,2,64,1280]{3,2,1,0:T(8,128)(2,1)}, u32[]{:S(2)}) copy-start(bf16[2,2,64,1280]{3,2,1,0:T(8,128)(2,1)} %copy-done.2) | copy-start | bytes 1966084
  183.9 74.1 %copy-start.6 = (f32[2,2,1280,32]{2,3,1,0:T(8,128)S(1)}, f32[2,2,1280,32]{2,3,1,0:T(8,128)}, u32[]{:S(2)}) copy-start(f32[2,2,1280,32]{2,3,1,0:T(8,128)} %fusion.101) | copy-start | bytes 1966084
  183.9 74.1 %copy-start.7 = (bf16[2,2,64,1280]{3,2,1,0:T(8,128)(2,1)S(1)}, bf16[2,2,64,1280]{3,2,1,0:T(8,128)(2,1)}, u32[]{:S(2)}) copy-start(bf16[2,2,64,1280]{3,2,1,0:T(8,128)(2,1)} %param.7) | copy-start | bytes 1966084
Sparse Core Ops, SparseCore 0:
  72.7 32.0 all-reduce.6
  108.2 91.1 all-reduce.8
